TPU v7x, 128 devices: a whole 4x4x4 slice. The times are simulated.
128 devices in a mesh: req: 8 (over y, core), exp: 16 (over z, x).
Axes of the slice: x: 4, y: 4, z: 4, core: 2. Of those that a mesh axis runs over, the one named last changes fastest.
Arguments:
- hidden: bfloat16 [16384, 2048], P(('req', 'exp')), may hold values from -6 to 6
- lengths: int32 [8, 4], P('req'), may hold values from 1 to 1536, 2048 in all within a row
- attn_gain: float32 [2048], replicated, may hold values from 0.25 to 1.75
- q_gain: float32 [128], replicated, may hold values from 1 to 4.5
- key_norm_gain: float32 [128], replicated, may hold values from 0.1 to 1.9
- w_query: bfloat16 [2048, 4096], P(None, 'exp'), may hold values from -0.125 to 0.125
- key_value_weight: bfloat16 [2048, 1024], replicated, may hold values from -0.125 to 0.125
- w_out: bfloat16 [4096, 2048], P('exp'), may hold values from -0.09375 to 0.09375
- ffn_gain: float32 [2048], replicated, may hold values from 0.25 to 1.75
- w_router: bfloat16 [2048, 128], replicated, may hold values from -0.125 to 0.125
- routes: int32 [16384, 8], P(('req', 'exp')), may hold values from 0 to 127, all different within a row; in each aligned block of 128 rows (0 to 127, 128 to 255, ...) at most 16 rows name the same one
- w_gate: bfloat16 [128, 2048, 768], P(('req', 'exp')), may hold values from -0.125 to 0.125
- w_up: bfloat16 [128, 2048, 768], P(('req', 'exp')), may hold values from -0.125 to 0.125
- w_down: bfloat16 [128, 768, 2048], P(('req', 'exp')), may hold values from -0.21875 to 0.21875
- page_table: int32 [1024], P(('req', 'exp')), may hold values from 0 to 1023, as said below
Outputs:
- layer_out: bfloat16 [16384, 2048], P(('req', 'exp'))
- kv_cache: bfloat16 [1024, 16384], P(('req', 'exp'))
Inputs may be any that keep to these rules, and one draw needn't show every extreme that they name: `routes`: in the rows of one device no expert is named more than 16 times. `page_table`: every page number appears exactly once. The blocks of the device with index (r, x) go to pages held by devices with exp index x, exactly (8) // 8 of them to each req index; the device with flat index i holds pages i * (8) onwards.
All inputs are finite; a program needn't handle non-finite values.
Results may differ from a plain program's by a relative error of at most 0.013.
Values may be sent and summed in bfloat16 or wider, within the bound.
A program may use at most 128 MiB of HBM per device.

v0:
```python
import math
import jax
import jax.numpy as jnp
from jax import lax
from jax.sharding import PartitionSpec as P

EPSILON = 1e-06
THETA_BASE = 1000000.0


def rms_norm(values, scale_gain):
    values = values.astype(jnp.float32)
    factor = lax.rsqrt(jnp.mean(values * values, -1, keepdims=True) + EPSILON)
    return values * factor * scale_gain


def rotate(values, positions):
    half_dim = values.shape[-1] // 2
    freqs = THETA_BASE ** (-jnp.arange(half_dim, dtype=jnp.float32) * 2.0 / values.shape[-1])
    angles = positions.astype(jnp.float32)[:, None] * freqs[None, :]
    cosine = jnp.cos(angles)[:, None, :]
    sine = jnp.sin(angles)[:, None, :]
    first_half = values[..., :half_dim]
    second_half = values[..., half_dim:]
    return jnp.concatenate(
        [first_half * cosine - second_half * sine, second_half * cosine + first_half * sine], -1
    )


def head_prepare(raw, scale_gain, positions, head_dim):
    row_count = raw.shape[0]
    split_heads = raw.reshape(row_count, raw.shape[1] // head_dim, head_dim)
    return (
        rotate(rms_norm(split_heads, scale_gain), positions)
        .reshape(row_count, raw.shape[1])
        .astype(jnp.bfloat16)
    )


def layout(prompt_lengths, row_count):
    ends = jnp.cumsum(prompt_lengths)
    starts = ends - prompt_lengths
    index = jnp.arange(row_count, dtype=jnp.int32)
    inside = (index[:, None] >= starts[None, :]) & (index[:, None] < ends[None, :])
    labels = jnp.arange(prompt_lengths.shape[0], dtype=jnp.int32)
    prompt = jnp.sum(jnp.where(inside, labels[None, :], 0), 1)
    token_position = index - jnp.sum(jnp.where(inside, starts[None, :], 0), 1)
    return (prompt, token_position)


def attend(query, key_rows, values_in, prompt, token_position, head_dim):
    row_count = query.shape[0]
    head_count = query.shape[1] // head_dim
    block_rows = min(512, row_count)
    block_list = row_count // block_rows
    query_blocks = query.reshape(block_list, block_rows, head_count, head_dim)

    def one_block(args):
        query_part, prompt_part, position_part = args
        scores = jnp.einsum(
            "qhd,kd->hqk", query_part, key_rows, preferred_element_type=jnp.float32
        ) / math.sqrt(head_dim)
        allowed = (prompt_part[:, None] == prompt[None, :]) & (
            token_position[None, :] <= position_part[:, None]
        )
        scores = jnp.where(allowed[None], scores, -1e30)
        highest = jnp.max(scores, -1, keepdims=True)
        weights = jnp.exp(scores - highest)
        soft = (weights / jnp.sum(weights, -1, keepdims=True)).astype(jnp.bfloat16)
        mixed = jnp.einsum("hqk,kd->qhd", soft, values_in, preferred_element_type=jnp.float32)
        return mixed.reshape(block_rows, head_count * head_dim).astype(jnp.bfloat16)

    result = lax.map(
        one_block,
        (
            query_blocks,
            prompt.reshape(block_list, block_rows),
            token_position.reshape(block_list, block_rows),
        ),
    )
    return result.reshape(row_count, head_count * head_dim)


def on_device(
    hidden,
    lengths,
    attn_gain,
    q_gain,
    key_norm_gain,
    w_query,
    key_value_weight,
    w_out,
    ffn_gain,
    w_router,
    routes,
    w_gate,
    w_up,
    w_down,
    page_table,
):
    head_dim = q_gain.shape[0]
    kv_heads = key_value_weight.shape[1] // (2 * head_dim)
    local_heads = w_query.shape[1] // head_dim
    query_heads = local_heads * lax.axis_size("exp")
    column = lax.axis_index("exp")
    tokens_here = hidden.shape[0]
    model_width = hidden.shape[1]
    group_rows = tokens_here * lax.axis_size("exp")
    normed = rms_norm(hidden, attn_gain).astype(jnp.bfloat16)
    prompt, token_position = layout(lengths[0], group_rows)
    own_position = lax.dynamic_slice_in_dim(token_position, column * tokens_here, tokens_here)
    key_value = jnp.dot(normed, key_value_weight, preferred_element_type=jnp.float32)
    own_keys = head_prepare(
        key_value[:, : kv_heads * head_dim], key_norm_gain, own_position, head_dim
    )
    own_rows = jnp.concatenate(
        [own_keys, key_value[:, kv_heads * head_dim :].astype(jnp.bfloat16)], 1
    )
    key_value_index = column * local_heads // (query_heads // kv_heads)
    key_cols = key_value_index * head_dim
    value_cols = key_cols + kv_heads * head_dim
    raw = jnp.dot(
        lax.all_gather(normed, "exp", axis=0, tiled=True),
        w_query,
        preferred_element_type=jnp.float32,
    )
    query = head_prepare(raw, q_gain, token_position, head_dim)
    every_row = lax.all_gather(own_rows, "exp", axis=0, tiled=True)
    key_rows = lax.dynamic_slice_in_dim(every_row, key_cols, head_dim, 1)
    value_rows_all = lax.dynamic_slice_in_dim(every_row, value_cols, head_dim, 1)
    mixed = attend(query, key_rows, value_rows_all, prompt, token_position, head_dim)
    projected = lax.psum_scatter(
        jnp.dot(mixed, w_out, preferred_element_type=jnp.float32).astype(jnp.bfloat16),
        "exp",
        scatter_dimension=0,
        tiled=True,
    ).astype(jnp.float32)
    resid = (hidden.astype(jnp.float32) + projected).astype(jnp.bfloat16)
    moe_in = rms_norm(resid, ffn_gain).astype(jnp.bfloat16)
    logits = jnp.dot(moe_in, w_router, preferred_element_type=jnp.float32)
    soft_router = jax.nn.softmax(logits, -1)
    expert_count = w_router.shape[1]
    top_count = routes.shape[1]
    chosen = routes[:, :, None] == jnp.arange(expert_count, dtype=jnp.int32)[None, None, :]
    picked = jnp.sum(jnp.where(chosen, soft_router[:, None, :], 0.0), -1)
    gates = picked / jnp.sum(picked, 1, keepdims=True)
    capacity = 2 * tokens_here * top_count // expert_count
    flat_chosen = chosen.reshape(tokens_here * top_count, expert_count).astype(jnp.int32)
    ranks = jnp.cumsum(flat_chosen, 0) - 1
    slot_ids = jnp.sum(ranks * flat_chosen, 1)
    target = routes.reshape(-1) * capacity + slot_ids
    source_rows = moe_in[jnp.arange(tokens_here * top_count, dtype=jnp.int32) // top_count]
    send_rows = (
        jnp.zeros((expert_count * capacity, model_width), jnp.bfloat16).at[target].set(source_rows)
    )
    direct = send_rows.reshape(expert_count, capacity, model_width)
    batch = lax.all_to_all(direct, ("req", "exp"), split_axis=0, concat_axis=0, tiled=True)
    batch_shape = batch.shape
    rows_flat = batch.reshape(-1, batch_shape[-1])
    gate_part = jnp.dot(rows_flat, w_gate[0], preferred_element_type=jnp.float32)
    up_part = jnp.dot(rows_flat, w_up[0], preferred_element_type=jnp.float32)
    act = (jax.nn.silu(gate_part) * up_part).astype(jnp.bfloat16)
    answer = jnp.dot(act, w_down[0], preferred_element_type=jnp.float32).astype(jnp.bfloat16)
    answered = answer.reshape(batch_shape[:-1] + (w_down.shape[2],))
    returned = lax.all_to_all(answered, ("req", "exp"), split_axis=0, concat_axis=0, tiled=True)
    outcome = returned.reshape(expert_count * capacity, model_width)[target]
    outcome = outcome.reshape(tokens_here, top_count, model_width)
    moe_sum = jnp.sum(outcome.astype(jnp.float32) * gates[:, :, None], 1)
    layer_out = (resid.astype(jnp.float32) + moe_sum).astype(jnp.bfloat16)
    blocks_here = page_table.shape[0]
    page_size = tokens_here // blocks_here
    page_width = page_size * own_rows.shape[1]
    page_blocks = own_rows.reshape(blocks_here, page_width)
    req_count = lax.axis_size("req")
    per_peer = blocks_here // req_count
    owner = page_table // blocks_here // lax.axis_size("exp")
    owner_hit = (owner[:, None] == jnp.arange(req_count, dtype=jnp.int32)[None, :]).astype(
        jnp.int32
    )
    rank_inside = jnp.sum((jnp.cumsum(owner_hit, 0) - 1) * owner_hit, 1)
    send_order = owner * per_peer + rank_inside
    send_pages = jnp.zeros_like(page_blocks).at[send_order].set(page_blocks)
    send_slots = jnp.zeros_like(page_table).at[send_order].set(page_table % blocks_here)
    got_pages, got_slots = (
        lax.all_to_all(
            send_pages.reshape(req_count, per_peer, page_width),
            "req",
            split_axis=0,
            concat_axis=0,
            tiled=True,
        ),
        lax.all_to_all(
            send_slots.reshape(req_count, per_peer), "req", split_axis=0, concat_axis=0, tiled=True
        ),
    )
    kv_cache = (
        jnp.zeros_like(page_blocks)
        .at[got_slots.reshape(-1)]
        .set(got_pages.reshape(blocks_here, page_width))
    )
    return (layer_out, kv_cache)


def solution(mesh):
    in_specs = (
        P(("req", "exp"), None),
        P("req", None),
        P(),
        P(),
        P(),
        P(None, "exp"),
        P(),
        P("exp", None),
        P(),
        P(),
        P(("req", "exp"), None),
        P(("req", "exp"), None, None),
        P(("req", "exp"), None, None),
        P(("req", "exp"), None, None),
        P(("req", "exp")),
    )
    out_specs = (P(("req", "exp"), None), P(("req", "exp"), None))
    return jax.shard_map(
        on_device, mesh=mesh, in_specs=in_specs, out_specs=out_specs, check_vma=False
    )
```

profile of v0, /device:TPU:60, one launch (start us, length us, event | category | flops | bytes accessed | tf_op | source)
XLA Modules:
  0.0 661.6 jit_solution(14308455975298828681)
XLA Ops:
  7.8 1.3 fusion.44
  9.2 2.0 fusion.46
  11.2 3.1 fusion.82
  23.9 6.3 multiply_cosine_fusion
  30.1 43.8 %all-gather.5.cloned.1.call-done = bf16[2048,1024]{1,0:T(8,128)(2,1)} async-done(((bf16[128,1024]{1,0:T(8,128)(2,1)}), bf16[2048,1024]{1,0:T(8,128)(2,1)}) %all-gather.5.cloned.1.call-update) | async-done | bytes 4194320 | tf_op jit(solution)/shard_map/all_gather | solution.py:128
  73.9 2.3 constant_dynamic-slice_fusion.2
  76.2 2.1 copy.88
  78.3 68.8 %all-gather.3.cloned.1.call-done = bf16[2048,2048]{1,0:T(8,128)(2,1)} async-done(((bf16[128,2048]{1,0:T(8,128)(2,1)}), bf16[2048,2048]{1,0:T(8,128)(2,1)}) %all-gather.3.cloned.1.call-update) | async-done | bytes 8388624 | tf_op jit(solution)/shard_map/all_gather | solution.py:123
  147.1 7.4 %multiply_reduce_fusion = (f32[2048,2]{0,1:T(2,128)S(1)}, f32[2048,256]{0,1:T(8,128)}) fusion(bf16[2048,2048]{1,0:T(8,128)(2,1)} %all-gather.3.cloned.1.call-done, bf16[2048,256]{1,0:T(8,128)(2,1)} %param.22), kind=kOutput, calls=%fused_computation.51 | convolution fusion | flops 2148528128 | bytes 11550720 | tf_op jit(solution)/shard_map/dot_general | solution.py:122
  154.5 2.9 copy.84
  157.5 2.1 multiply_multiply_fusion
  160.4 1.6 pad_maximum_fusion
  162.1 69.5 %while.10 = (s32[]{:T(128)}, bf16[4,512,256]{2,1,0:T(8,128)(2,1)}, s32[4,512]{1,0:T(4,128)S(1)}, s32[2048]{0:T(1024)S(1)}, s32[2048]{0:T(1024)S(1)}, /*index=5*/...) while((s32[]{:T(128)}, bf16[4,512,256]{2,1,0:T(8,128)(2,1)}, ...), condition=%wide.region_9.10_spmd, body=%wide.region_6.9_spmd.sunk | while | flops 1089603584 | bytes 21532792 | solution.py:73
  162.1 1.9 compare_and_fusion.2
  164.0 7.9 %fusion.101 = (f32[2,512]{1,0:T(2,128)S(1)}, f32[2,512,2048]{2,1,0:T(8,128)}) fusion(pred[512,2048]{1,0:T(8,128)(4,1)} %compare_and_fusion.2, bf16[2048,128]{1,0:T(8,128)(2,1)} %get-tuple-element.247, bf16[4,512,2,128]{3,1,0,2:T(8,128)(2,1)} %get-tuple-element.246, s32[]{:T(128)S(6)} %copy.117), kind=kOutput, calls=%fused_computation.146.clone.1 | convolution fusion | flops 545261568 | bytes 10227716 | tf_op jit(solution)/shard_map/while/body/eval_jaxpr/sub | solution.py:68
  171.8 5.7 fusion.102
  177.6 1.1 copy.113
  179.4 1.9 compare_and_fusion.2
  181.3 7.9 %fusion.101 = (f32[2,512]{1,0:T(2,128)S(1)}, f32[2,512,2048]{2,1,0:T(8,128)}) fusion(pred[512,2048]{1,0:T(8,128)(4,1)} %compare_and_fusion.2, bf16[2048,128]{1,0:T(8,128)(2,1)} %get-tuple-element.247, bf16[4,512,2,128]{3,1,0,2:T(8,128)(2,1)} %get-tuple-element.246, s32[]{:T(128)S(6)} %copy.117), kind=kOutput, calls=%fused_computation.146.clone.1 | convolution fusion | flops 545261568 | bytes 10227716 | tf_op jit(solution)/shard_map/while/body/eval_jaxpr/sub | solution.py:68
  189.2 5.7 fusion.102
  194.9 1.1 copy.113
  196.7 1.9 compare_and_fusion.2
  198.6 7.9 %fusion.101 = (f32[2,512]{1,0:T(2,128)S(1)}, f32[2,512,2048]{2,1,0:T(8,128)}) fusion(pred[512,2048]{1,0:T(8,128)(4,1)} %compare_and_fusion.2, bf16[2048,128]{1,0:T(8,128)(2,1)} %get-tuple-element.247, bf16[4,512,2,128]{3,1,0,2:T(8,128)(2,1)} %get-tuple-element.246, s32[]{:T(128)S(6)} %copy.117), kind=kOutput, calls=%fused_computation.146.clone.1 | convolution fusion | flops 545261568 | bytes 10227716 | tf_op jit(solution)/shard_map/while/body/eval_jaxpr/sub | solution.py:68
  206.5 5.7 fusion.102
  214.1 1.9 compare_and_fusion.2
  215.9 7.9 %fusion.101 = (f32[2,512]{1,0:T(2,128)S(1)}, f32[2,512,2048]{2,1,0:T(8,128)}) fusion(pred[512,2048]{1,0:T(8,128)(4,1)} %compare_and_fusion.2, bf16[2048,128]{1,0:T(8,128)(2,1)} %get-tuple-element.247, bf16[4,512,2,128]{3,1,0,2:T(8,128)(2,1)} %get-tuple-element.246, s32[]{:T(128)S(6)} %copy.117), kind=kOutput, calls=%fused_computation.146.clone.1 | convolution fusion | flops 545261568 | bytes 10227716 | tf_op jit(solution)/shard_map/while/body/eval_jaxpr/sub | solution.py:68
  223.8 5.7 fusion.102
  231.5 7.1 %convolution_convert_fusion.1 = bf16[2048,2048]{1,0:T(8,128)(2,1)} fusion(bf16[2048,256]{1,0:T(8,128)(2,1)} %bitcast.130, bf16[256,2048]{1,0:T(8,128)(2,1)} %param.24), kind=kOutput, calls=%fused_computation.38 | convolution fusion | flops 2151677952 | bytes 10485760 | tf_op jit(solution)/shard_map/dot_general | solution.py:133
  242.6 80.9 %reduce-scatter.2.cloned.1.call-done = bf16[128,2048]{1,0:T(8,128)(2,1)} async-done(((bf16[2048,2048]{1,0:T(8,128)(2,1)}), bf16[128,2048]{1,0:T(8,128)(2,1)}) %reduce-scatter.2.cloned.1.call-update) | async-done | bytes 524304 | tf_op jit(solution)/shard_map/reduce_scatter | solution.py:132
  323.4 1.5 fusion.48
  324.9 2.2 fusion.50
  327.1 25.1 %scatter_custom_fusion = bf16[2048,2048]{1,0:T(8,128)(2,1)} fusion(s32[1024]{0:T(1024)S(1)} %bitcast.138, bf16[128,2048]{1,0:T(8,128)(2,1)} %fusion.50, s32[1024]{0:T(1024)S(1)} %broadcast_clamp_fusion.1, bf16[]{:T(256)} %constant.128.clone.1), kind=kCustom, calls=%fused_computation.40 | custom fusion | bytes 8389120 | tf_op jit(solution)/shard_map/scatter | solution.py:154
  352.1 9.7 %all-to-all-start = ((bf16[128,16,2048]{2,1,0:T(8,128)(2,1)}), bf16[128,16,2048]{2,1,0:T(8,128)(2,1)}, u32[]{:S(2)}, u32[]{:S(2)}) async-start(bf16[128,16,2048]{2,1,0:T(8,128)(2,1)} %bitcast.126), calls=%async_computation.1 | async-start | bytes 16777216 | tf_op jit(solution)/shard_map/all_to_all | solution.py:157
  364.5 1.4 scatter_custom_fusion.2
  366.5 1.4 reduce.2
  367.9 1.9 reshape.501
  369.7 102.7 %all-to-all-done = bf16[128,16,2048]{2,1,0:T(8,128)(2,1)} async-done(((bf16[128,16,2048]{2,1,0:T(8,128)(2,1)}), bf16[128,16,2048]{2,1,0:T(8,128)(2,1)}, u32[]{:S(2)}, u32[]{:S(2)}) %all-to-all-start) | async-done | bytes 8388640 | tf_op jit(solution)/shard_map/all_to_all | solution.py:157
  472.4 4.5 all-to-all-start.2
  476.9 11.7 %fusion.41 = f32[2048,768]{1,0:T(8,128)} fusion(bf16[2048,2048]{1,0:T(8,128)(2,1)} %bitcast.22, bf16[1,2048,768]{2,1,0:T(8,128)(2,1)} %param.28), kind=kOutput, calls=%fused_computation.45 | convolution fusion | flops 6442450944 | bytes 17825792 | tf_op jit(solution)/shard_map/dot_general | solution.py:160
  488.6 4.8 all-to-all-start.3
  493.4 21.3 %convolution_convert_fusion = bf16[2048,2048]{1,0:T(8,128)(2,1)} fusion(f32[2048,768]{1,0:T(8,128)} %fusion.41, bf16[2048,2048]{1,0:T(8,128)(2,1)} %bitcast.22, bf16[1,768,2048]{2,1,0:T(8,128)(2,1)S(1)} %copy-done, bf16[1,2048,768]{2,1,0:T(8,128)(2,1)} %param.29), kind=kOutput, calls=%fused_computation.37 | convolution fusion | flops 12898533376 | bytes 29360128 | tf_op jit(solution)/shard_map/dot_general | solution.py:163
  514.7 8.5 %all-to-all-start.1 = ((bf16[128,16,2048]{2,1,0:T(8,128)(2,1)}), bf16[128,16,2048]{2,1,0:T(8,128)(2,1)}, u32[]{:S(2)}, u32[]{:S(2)}) async-start(bf16[128,16,2048]{2,1,0:T(8,128)(2,1)} %bitcast.127), calls=%async_computation.2 | async-start | bytes 16777216 | tf_op jit(solution)/shard_map/all_to_all | solution.py:165
  524.4 2.6 scatter_custom_fusion.3
  527.1 1.6 fusion.81
  528.8 2.0 select_reduce_fusion
  530.9 102.8 %all-to-all-done.1 = bf16[128,16,2048]{2,1,0:T(8,128)(2,1)} async-done(((bf16[128,16,2048]{2,1,0:T(8,128)(2,1)}), bf16[128,16,2048]{2,1,0:T(8,128)(2,1)}, u32[]{:S(2)}, u32[]{:S(2)}) %all-to-all-start.1) | async-done | bytes 8388640 | tf_op jit(solution)/shard_map/all_to_all | solution.py:165
  633.7 13.3 %gather_fusion = bf16[1024,2048]{1,0:T(8,128)(2,1)} fusion(bf16[2048,2048]{1,0:T(8,128)(2,1)} %bitcast.27, s32[1024]{0:T(1024)S(1)} %broadcast_clamp_fusion), kind=kCustom, calls=%fused_computation.1 | custom fusion | bytes 8392704 | tf_op jit(solution)/shard_map/gather | solution.py:166
  647.0 6.6 fusion.34
  (104 shorter events, 25.5 us)
Async XLA Ops:
  7.2 486.3 %copy-start = (bf16[1,768,2048]{2,1,0:T(8,128)(2,1)S(1)}, bf16[1,768,2048]{2,1,0:T(8,128)(2,1)}, u32[]{:S(2)}) copy-start(bf16[1,768,2048]{2,1,0:T(8,128)(2,1)} %param.30) | copy-start | bytes 9437188
  7.2 7.8 %copy-start.11 = (s32[1,4]{1,0:T(1,128)S(1)}, s32[1,4]{1,0:T(1,128)}, u32[]{:S(2)}) copy-start(s32[1,4]{1,0:T(1,128)} %param.18) | copy-start | bytes 52
  7.2 66.7 %all-gather.5.cloned.1.call-start = ((), (), s32[]{:S(2)}) async-start(), calls=%async_computation.6 | async-start | bytes 4456448 | tf_op jit(solution)/shard_map/all_gather | solution.py:128
  15.3 0.6 copy-start.7
  21.8 125.3 %all-gather.3.cloned.1.call-start = ((), (), s32[]{:S(2)}) async-start(), calls=%async_computation.5 | async-start | bytes 8912896 | tf_op jit(solution)/shard_map/all_gather | solution.py:123
  22.6 300.9 %reduce-scatter.2.cloned.1.call-start = ((), (), s32[]{:S(2)}) async-start(), calls=%async_computation.7 | async-start | bytes 8912896 | tf_op jit(solution)/shard_map/reduce_scatter | solution.py:132
  154.5 3.0 copy-start.10
  157.5 2.1 copy-start.3
  157.5 2.2 copy-start.4
  238.6 0.7 copy-start.8
  239.3 85.6 %copy-start.9 = (f32[2048]{0:T(1024)S(1)}, f32[2048]{0:T(1024)}, u32[]{:S(2)}) copy-start(f32[2048]{0:T(1024)} %param.25) | copy-start | bytes 24580
  240.1 0.8 copy-start.6
  352.1 9.8 %copy-start.5 = (bf16[128,1024]{1,0:T(8,128)(2,1)S(1)}, bf16[128,1024]{1,0:T(8,128)(2,1)}, u32[]{:S(2)}) copy-start(bf16[128,1024]{1,0:T(8,128)(2,1)} %pad_maximum_fusion.1) | copy-start | bytes 786436
  352.1 10.6 %copy-start.12 = (s32[8]{0:T(128)S(1)}, s32[8]{0:T(128)}, u32[]{:S(2)}) copy-start(s32[8]{0:T(128)} %param.31) | copy-start | bytes 100
  352.1 120.3 %all-to-all-start = ((bf16[128,16,2048]{2,1,0:T(8,128)(2,1)}), bf16[128,16,2048]{2,1,0:T(8,128)(2,1)}, u32[]{:S(2)}, u32[]{:S(2)}) async-start(bf16[128,16,2048]{2,1,0:T(8,128)(2,1)} %bitcast.126), calls=%async_computation.1 | async-start | bytes 16777216 | tf_op jit(solution)/shard_map/all_to_all | solution.py:157
  472.4 16.2 %all-to-all-start.2 = ((s32[8,1,1]{2,1,0:T(1,128)}), s32[8,1,1]{2,1,0:T(1,128)S(1)}, u32[]{:S(2)}, u32[]{:S(2)}) async-start(s32[8,1,1]{2,1,0:T(1,128)} %copy.97), calls=%async_computation.3 | async-start | bytes 8192 | tf_op jit(solution)/shard_map/all_to_all | solution.py:192
  488.6 26.1 %all-to-all-start.3 = ((bf16[8,2,8192]{2,1,0:T(2,128)(2,1)}), bf16[8,2,8192]{2,1,0:T(2,128)(2,1)S(1)}, u32[]{:S(2)}, u32[]{:S(2)}) async-start(bf16[8,2,8192]{2,1,0:T(2,128)(2,1)} %reshape.501), calls=%async_computation.4 | async-start | bytes 524288 | tf_op jit(solution)/shard_map/all_to_all | solution.py:185
  514.7 119.1 %all-to-all-start.1 = ((bf16[128,16,2048]{2,1,0:T(8,128)(2,1)}), bf16[128,16,2048]{2,1,0:T(8,128)(2,1)}, u32[]{:S(2)}, u32[]{:S(2)}) async-start(bf16[128,16,2048]{2,1,0:T(8,128)(2,1)} %bitcast.127), calls=%async_computation.2 | async-start | bytes 16777216 | tf_op jit(solution)/shard_map/all_to_all | solution.py:165
  647.0 6.6 copy-start.1
  647.0 6.6 %copy-start.2 = (bf16[128,2048]{1,0:T(8,128)(2,1)S(1)}, bf16[128,2048]{1,0:T(8,128)(2,1)}, u32[]{:S(2)}) copy-start(bf16[128,2048]{1,0:T(8,128)(2,1)} %reduce-scatter.2.cloned.1.call-done) | copy-start | bytes 1572868
Sparse Core Ops, SparseCore 0:
  21.9 51.9 all-gather.4
  76.6 70.4 all-gather.2
  238.8 84.5 reduce-scatter.1
where the time goes:
time: 666 us; the launch traced here: 662 us
  waiting for transfers between devices  400 us (60%)
  matrix products  106 us (16%)
  local copies, waits for them, and re-layouts  68.1 us (10%)
  other arithmetic  44.4 us (7%)
  starting transfers between devices  28.2 us (4%)
  between operations  14.5 us (2%)
    all_to_all x1, waiting for transfers between devices, on_device(): lax.all_to_all(answered, ('req', 'exp'), split_axis=0, concat_axis=0, til...  103 us
    all_to_all x1, waiting for transfers between devices, on_device(): lax.all_to_all(direct, ('req', 'exp'), split_axis=0, concat_axis=0, tiled...  103 us
    reduce_scatter x1, waiting for transfers between devices, on_device(): lax.psum_scatter(jnp.dot(mixed, w_out, preferred_element_type=jnp.float32...  80.9 us
    all_gather x1, waiting for transfers between devices, on_device(): lax.all_gather(normed, 'exp', axis=0, tiled=True)  68.8 us
    all_gather x1, waiting for transfers between devices, on_device(): every_row = lax.all_gather(own_rows, 'exp', axis=0, tiled=True)  43.8 us
    sub x4, matrix products, one_block(): weights = jnp.exp(scores - highest)  31.5 us
    scatter x1, local copies, waits for them, and re-layouts, on_device(): jnp.zeros((expert_count * capacity, model_width), jnp.bfloat16).at[target]  25.1 us
    dot_general x4, matrix products, one_block(): jnp.einsum('hqk,kd->qhd', soft, values_in, preferred_element_type=jnp.flo...  22.9 us
  transfers between devices with their start and end apart: 7, of which 5 were waited for; matrix products, arithmetic and copies ran while one was open for 9% of the time, Pallas kernels for 0%

commit v1 on v0

--- a/solution.py
+++ b/solution.py
@@ -120,7 +120,15 @@
     key_cols = key_value_index * head_dim
     value_cols = key_cols + kv_heads * head_dim
     raw = jnp.dot(
-        lax.all_gather(normed, "exp", axis=0, tiled=True),
+        jnp.concatenate(
+            lax.all_to_all(
+                jnp.stack([normed] * lax.axis_size("exp"), axis=0),
+                axis_name="exp",
+                split_axis=0,
+                concat_axis=0,
+            ),
+            0,
+        ),
         w_query,
         preferred_element_type=jnp.float32,
     )

time: 666 us -> 699 us (1.050)
  waiting for transfers between devices: 400 us -> 421 us
  local copies, waits for them, and re-layouts: 68.1 us -> 78 us
  starting transfers between devices: 28.2 us -> 36.1 us
    all_gather x1, waiting for transfers between devices: 43.8 us -> 132 us  [on_device(): every_row = lax.all_gather(own_rows, 'exp', axis=0, tiled=True)]
    all_gather x1 -> x0, waiting for transfers between devices: 68.8 us -> none  [on_device(): lax.all_gather(normed, 'exp', axis=0, tiled=True)]
    all_to_all x0 -> x1, starting transfers between devices: none -> 7.97 us  [on_device(): lax.all_to_all(jnp.stack([normed] * lax.axis_size('exp'), axis=0), axis_n...]
  transfers between devices with their start and end apart: 7 -> 7, of which waited for: 5 -> 4; matrix products, arithmetic and copies ran while one was open for 9% -> 9% of each run, Pallas kernels for 0% -> 0%
where the time goes in v1:
time: 699 us; the launch traced here: 694 us
  waiting for transfers between devices  421 us (60%)
  matrix products  105 us (15%)
  local copies, waits for them, and re-layouts  78 us (11%)
  other arithmetic  38.5 us (6%)
  starting transfers between devices  36.1 us (5%)
  between operations  14.9 us (2%)
    all_gather x1, waiting for transfers between devices, on_device(): every_row = lax.all_gather(own_rows, 'exp', axis=0, tiled=True)  132 us
    all_to_all x1, waiting for transfers between devices, on_device(): lax.all_to_all(answered, ('req', 'exp'), split_axis=0, concat_axis=0, til...  103 us
    all_to_all x1, waiting for transfers between devices, on_device(): lax.all_to_all(direct, ('req', 'exp'), split_axis=0, concat_axis=0, tiled...  103 us
    reduce_scatter x1, waiting for transfers between devices, on_device(): lax.psum_scatter(jnp.dot(mixed, w_out, preferred_element_type=jnp.float32...  83.3 us
    sub x4, matrix products, one_block(): weights = jnp.exp(scores - highest)  31.5 us
    scatter x1, local copies, waits for them, and re-layouts, on_device(): jnp.zeros((expert_count * capacity, model_width), jnp.bfloat16).at[target]  25.1 us
    dot_general x4, matrix products, one_block(): jnp.einsum('hqk,kd->qhd', soft, values_in, preferred_element_type=jnp.flo...  22.9 us
    dot_general x1, matrix products, on_device(): jnp.dot(act, w_down[0], preferred_element_type=jnp.float32)  21.3 us
  transfers between devices with their start and end apart: 7, of which 4 were waited for; matrix products, arithmetic and copies ran while one was open for 9% of the time, Pallas kernels for 0%

profile of v1, /device:TPU:60, one launch (start us, length us, event | category | flops | bytes accessed | tf_op | source)
XLA Modules:
  0.0 694.1 jit_solution(7561252231989651260)
XLA Ops:
  7.8 1.3 fusion.44
  9.1 1.2 fusion.46
  11.1 2.9 fusion.82
  21.5 5.3 stack.2
  26.9 8.0 %all-to-all-start = ((bf16[16,128,2048]{2,1,0:T(8,128)(2,1)}), bf16[16,128,2048]{2,1,0:T(8,128)(2,1)}, u32[]{:S(2)}, u32[]{:S(2)}) async-start(bf16[16,128,2048]{2,1,0:T(8,128)(2,1)} %stack.2), calls=%async_computation | async-start | bytes 16777216 | tf_op jit(solution)/shard_map/all_to_all | solution.py:124
  35.5 2.3 copy.101
  37.8 2.8 multiply_cosine_fusion
  40.6 132.4 %all-gather.2.cloned.1.call-done = bf16[2048,1024]{1,0:T(8,128)(2,1)} async-done(((bf16[128,1024]{1,0:T(8,128)(2,1)}), bf16[2048,1024]{1,0:T(8,128)(2,1)}) %all-gather.2.cloned.1.call-update) | async-done | bytes 4194320 | tf_op jit(solution)/shard_map/all_gather | solution.py:136
  173.0 2.3 constant_dynamic-slice_fusion.2
  175.3 2.0 copy.90
  177.4 6.1 multiply_reduce_fusion
  185.4 2.6 convert_element_type.88
  188.0 2.7 copy.89
  190.7 69.4 %while.10 = (s32[]{:T(128)}, bf16[4,512,256]{2,1,0:T(8,128)(2,1)}, s32[4,512]{1,0:T(4,128)S(1)}, s32[2048]{0:T(1024)S(1)}, s32[2048]{0:T(1024)S(1)}, /*index=5*/...) while((s32[]{:T(128)}, bf16[4,512,256]{2,1,0:T(8,128)(2,1)}, ...), condition=%wide.region_9.10_spmd, body=%wide.region_6.9_spmd.sunk | while | flops 1089603584 | bytes 21532792 | solution.py:73
  190.7 1.9 compare_and_fusion.2
  192.6 7.9 %fusion.101 = (f32[2,512]{1,0:T(2,128)S(1)}, f32[2,512,2048]{2,1,0:T(8,128)}) fusion(pred[512,2048]{1,0:T(8,128)(4,1)} %compare_and_fusion.2, bf16[2048,128]{1,0:T(8,128)(2,1)} %get-tuple-element.247, bf16[4,512,2,128]{3,1,2,0:T(8,128)(2,1)} %get-tuple-element.246, s32[]{:T(128)S(6)} %copy.119), kind=kOutput, calls=%fused_computation.146.clone.1 | convolution fusion | flops 545261568 | bytes 10227716 | tf_op jit(solution)/shard_map/while/body/eval_jaxpr/sub | solution.py:68
  200.5 5.7 fusion.102
  208.0 1.9 compare_and_fusion.2
  209.9 7.9 %fusion.101 = (f32[2,512]{1,0:T(2,128)S(1)}, f32[2,512,2048]{2,1,0:T(8,128)}) fusion(pred[512,2048]{1,0:T(8,128)(4,1)} %compare_and_fusion.2, bf16[2048,128]{1,0:T(8,128)(2,1)} %get-tuple-element.247, bf16[4,512,2,128]{3,1,2,0:T(8,128)(2,1)} %get-tuple-element.246, s32[]{:T(128)S(6)} %copy.119), kind=kOutput, calls=%fused_computation.146.clone.1 | convolution fusion | flops 545261568 | bytes 10227716 | tf_op jit(solution)/shard_map/while/body/eval_jaxpr/sub | solution.py:68
  217.8 5.7 fusion.102
  225.3 1.9 compare_and_fusion.2
  227.2 7.9 %fusion.101 = (f32[2,512]{1,0:T(2,128)S(1)}, f32[2,512,2048]{2,1,0:T(8,128)}) fusion(pred[512,2048]{1,0:T(8,128)(4,1)} %compare_and_fusion.2, bf16[2048,128]{1,0:T(8,128)(2,1)} %get-tuple-element.247, bf16[4,512,2,128]{3,1,2,0:T(8,128)(2,1)} %get-tuple-element.246, s32[]{:T(128)S(6)} %copy.119), kind=kOutput, calls=%fused_computation.146.clone.1 | convolution fusion | flops 545261568 | bytes 10227716 | tf_op jit(solution)/shard_map/while/body/eval_jaxpr/sub | solution.py:68
  235.1 5.7 fusion.102
  242.6 1.9 compare_and_fusion.2
  244.5 7.9 %fusion.101 = (f32[2,512]{1,0:T(2,128)S(1)}, f32[2,512,2048]{2,1,0:T(8,128)}) fusion(pred[512,2048]{1,0:T(8,128)(4,1)} %compare_and_fusion.2, bf16[2048,128]{1,0:T(8,128)(2,1)} %get-tuple-element.247, bf16[4,512,2,128]{3,1,2,0:T(8,128)(2,1)} %get-tuple-element.246, s32[]{:T(128)S(6)} %copy.119), kind=kOutput, calls=%fused_computation.146.clone.1 | convolution fusion | flops 545261568 | bytes 10227716 | tf_op jit(solution)/shard_map/while/body/eval_jaxpr/sub | solution.py:68
  252.4 5.7 fusion.102
  260.1 7.1 %convolution_convert_fusion.1 = bf16[2048,2048]{1,0:T(8,128)(2,1)} fusion(bf16[2048,256]{1,0:T(8,128)(2,1)} %bitcast.131, bf16[256,2048]{1,0:T(8,128)(2,1)} %param.24), kind=kOutput, calls=%fused_computation.38 | convolution fusion | flops 2151677952 | bytes 10485760 | tf_op jit(solution)/shard_map/dot_general | solution.py:141
  271.1 83.3 %reduce-scatter.2.cloned.1.call-done = bf16[128,2048]{1,0:T(8,128)(2,1)} async-done(((bf16[2048,2048]{1,0:T(8,128)(2,1)}), bf16[128,2048]{1,0:T(8,128)(2,1)}) %reduce-scatter.2.cloned.1.call-update) | async-done | bytes 524304 | tf_op jit(solution)/shard_map/reduce_scatter | solution.py:140
  354.5 1.5 fusion.48
  356.0 2.2 fusion.50
  358.2 25.1 %scatter_custom_fusion = bf16[2048,2048]{1,0:T(8,128)(2,1)} fusion(s32[1024]{0:T(1024)S(1)} %bitcast.140, bf16[128,2048]{1,0:T(8,128)(2,1)} %fusion.50, s32[1024]{0:T(1024)S(1)} %broadcast_clamp_fusion.1, bf16[]{:T(256)} %constant.128.clone.1), kind=kCustom, calls=%fused_computation.40 | custom fusion | bytes 8389120 | tf_op jit(solution)/shard_map/scatter | solution.py:162
  383.2 9.7 %all-to-all-start.1 = ((bf16[128,16,2048]{2,1,0:T(8,128)(2,1)}), bf16[128,16,2048]{2,1,0:T(8,128)(2,1)}, u32[]{:S(2)}, u32[]{:S(2)}) async-start(bf16[128,16,2048]{2,1,0:T(8,128)(2,1)} %bitcast.128), calls=%async_computation.2 | async-start | bytes 16777216 | tf_op jit(solution)/shard_map/all_to_all | solution.py:165
  395.6 1.4 scatter_custom_fusion.2
  397.5 1.4 reduce.2
  398.9 1.9 reshape.506
  400.8 102.7 %all-to-all-done.1 = bf16[128,16,2048]{2,1,0:T(8,128)(2,1)} async-done(((bf16[128,16,2048]{2,1,0:T(8,128)(2,1)}), bf16[128,16,2048]{2,1,0:T(8,128)(2,1)}, u32[]{:S(2)}, u32[]{:S(2)}) %all-to-all-start.1) | async-done | bytes 8388640 | tf_op jit(solution)/shard_map/all_to_all | solution.py:165
  503.5 4.5 all-to-all-start.3
  508.0 11.7 %fusion.41 = f32[2048,768]{1,0:T(8,128)} fusion(bf16[2048,2048]{1,0:T(8,128)(2,1)} %bitcast.24, bf16[1,2048,768]{2,1,0:T(8,128)(2,1)} %param.28), kind=kOutput, calls=%fused_computation.45 | convolution fusion | flops 6442450944 | bytes 17825792 | tf_op jit(solution)/shard_map/dot_general | solution.py:168
  519.7 4.8 all-to-all-start.4
  524.5 21.3 %convolution_convert_fusion = bf16[2048,2048]{1,0:T(8,128)(2,1)} fusion(f32[2048,768]{1,0:T(8,128)} %fusion.41, bf16[2048,2048]{1,0:T(8,128)(2,1)} %bitcast.24, bf16[1,768,2048]{2,1,0:T(8,128)(2,1)S(1)} %copy-done, bf16[1,2048,768]{2,1,0:T(8,128)(2,1)} %param.29), kind=kOutput, calls=%fused_computation.37 | convolution fusion | flops 12898533376 | bytes 29360128 | tf_op jit(solution)/shard_map/dot_general | solution.py:171
  545.8 8.5 %all-to-all-start.2 = ((bf16[128,16,2048]{2,1,0:T(8,128)(2,1)}), bf16[128,16,2048]{2,1,0:T(8,128)(2,1)}, u32[]{:S(2)}, u32[]{:S(2)}) async-start(bf16[128,16,2048]{2,1,0:T(8,128)(2,1)} %bitcast.129), calls=%async_computation.3 | async-start | bytes 16777216 | tf_op jit(solution)/shard_map/all_to_all | solution.py:173
  555.5 2.6 scatter_custom_fusion.3
  558.1 1.6 fusion.81
  559.9 2.0 select_reduce_fusion
  562.0 102.8 %all-to-all-done.2 = bf16[128,16,2048]{2,1,0:T(8,128)(2,1)} async-done(((bf16[128,16,2048]{2,1,0:T(8,128)(2,1)}), bf16[128,16,2048]{2,1,0:T(8,128)(2,1)}, u32[]{:S(2)}, u32[]{:S(2)}) %all-to-all-start.2) | async-done | bytes 8388640 | tf_op jit(solution)/shard_map/all_to_all | solution.py:173
  664.8 13.3 %gather_fusion = bf16[1024,2048]{1,0:T(8,128)(2,1)} fusion(bf16[2048,2048]{1,0:T(8,128)(2,1)} %bitcast.29, s32[1024]{0:T(1024)S(1)} %broadcast_clamp_fusion), kind=kCustom, calls=%fused_computation.1 | custom fusion | bytes 8392704 | tf_op jit(solution)/shard_map/gather | solution.py:174
  678.1 6.5 fusion.34
  684.6 2.2 fusion.51
  (110 shorter events, 26.9 us)
Async XLA Ops:
  7.2 517.3 %copy-start = (bf16[1,768,2048]{2,1,0:T(8,128)(2,1)S(1)}, bf16[1,768,2048]{2,1,0:T(8,128)(2,1)}, u32[]{:S(2)}) copy-start(bf16[1,768,2048]{2,1,0:T(8,128)(2,1)} %param.30) | copy-start | bytes 9437188
  7.2 7.6 %copy-start.13 = (s32[1,4]{1,0:T(1,128)S(1)}, s32[1,4]{1,0:T(1,128)}, u32[]{:S(2)}) copy-start(s32[1,4]{1,0:T(1,128)} %param.18) | copy-start | bytes 52
  7.2 165.8 %all-gather.2.cloned.1.call-start = ((), (), s32[]{:S(2)}) async-start(), calls=%async_computation.6 | async-start | bytes 4456448 | tf_op jit(solution)/shard_map/all_gather | solution.py:136
  10.3 0.8 copy-start.1
  15.1 0.6 copy-start.6
  26.8 8.6 %copy-start.7 = (s32[2048]{0:T(1024)S(1)}, s32[2048]{0:T(1024)}, u32[]{:S(2)}) copy-start(s32[2048]{0:T(1024)} %copy-done.6) | copy-start | bytes 24580
  26.9 10.9 %copy-start.8 = (f32[2048]{0:T(1024)S(1)}, f32[2048]{0:T(1024)}, u32[]{:S(2)}) copy-start(f32[2048]{0:T(1024)} %get-tuple-element.147) | copy-start | bytes 24580
  26.9 10.9 %copy-start.11 = (f32[64]{0:T(128)S(1)}, f32[64]{0:T(128)}, u32[]{:S(2)}) copy-start(f32[64]{0:T(128)} %multiply_power_fusion) | copy-start | bytes 772
  26.9 150.5 %all-to-all-start = ((bf16[16,128,2048]{2,1,0:T(8,128)(2,1)}), bf16[16,128,2048]{2,1,0:T(8,128)(2,1)}, u32[]{:S(2)}, u32[]{:S(2)}) async-start(bf16[16,128,2048]{2,1,0:T(8,128)(2,1)} %stack.2), calls=%async_computation | async-start | bytes 16777216 | tf_op jit(solution)/shard_map/all_to_all | solution.py:124
  34.8 319.7 %reduce-scatter.2.cloned.1.call-start = ((), (), s32[]{:S(2)}) async-start(), calls=%async_computation.7 | async-start | bytes 8912896 | tf_op jit(solution)/shard_map/reduce_scatter | solution.py:140
  177.4 6.1 copy-start.12
  177.4 6.5 copy-start.4
  177.4 6.5 copy-start.5
  267.2 0.7 copy-start.9
  267.2 88.7 %copy-start.10 = (f32[2048]{0:T(1024)S(1)}, f32[2048]{0:T(1024)}, u32[]{:S(2)}) copy-start(f32[2048]{0:T(1024)} %param.25) | copy-start | bytes 24580
  268.7 0.8 copy-start.3
  383.2 9.7 %copy-start.2 = (bf16[128,1024]{1,0:T(8,128)(2,1)S(1)}, bf16[128,1024]{1,0:T(8,128)(2,1)}, u32[]{:S(2)}) copy-start(bf16[128,1024]{1,0:T(8,128)(2,1)} %pad_maximum_fusion.1) | copy-start | bytes 786436
  383.2 10.6 %copy-start.14 = (s32[8]{0:T(128)S(1)}, s32[8]{0:T(128)}, u32[]{:S(2)}) copy-start(s32[8]{0:T(128)} %param.31) | copy-start | bytes 100
  383.2 120.3 %all-to-all-start.1 = ((bf16[128,16,2048]{2,1,0:T(8,128)(2,1)}), bf16[128,16,2048]{2,1,0:T(8,128)(2,1)}, u32[]{:S(2)}, u32[]{:S(2)}) async-start(bf16[128,16,2048]{2,1,0:T(8,128)(2,1)} %bitcast.128), calls=%async_computation.2 | async-start | bytes 16777216 | tf_op jit(solution)/shard_map/all_to_all | solution.py:165
  503.5 16.2 %all-to-all-start.3 = ((s32[8,1,1]{2,1,0:T(1,128)}), s32[8,1,1]{2,1,0:T(1,128)S(1)}, u32[]{:S(2)}, u32[]{:S(2)}) async-start(s32[8,1,1]{2,1,0:T(1,128)} %copy.99), calls=%async_computation.4 | async-start | bytes 8192 | tf_op jit(solution)/shard_map/all_to_all | solution.py:200
  519.7 26.1 %all-to-all-start.4 = ((bf16[8,2,8192]{2,1,0:T(2,128)(2,1)}), bf16[8,2,8192]{2,1,0:T(2,128)(2,1)S(1)}, u32[]{:S(2)}, u32[]{:S(2)}) async-start(bf16[8,2,8192]{2,1,0:T(2,128)(2,1)} %reshape.506), calls=%async_computation.5 | async-start | bytes 524288 | tf_op jit(solution)/shard_map/all_to_all | solution.py:193
  545.8 119.0 %all-to-all-start.2 = ((bf16[128,16,2048]{2,1,0:T(8,128)(2,1)}), bf16[128,16,2048]{2,1,0:T(8,128)(2,1)}, u32[]{:S(2)}, u32[]{:S(2)}) async-start(bf16[128,16,2048]{2,1,0:T(8,128)(2,1)} %bitcast.129), calls=%async_computation.3 | async-start | bytes 16777216 | tf_op jit(solution)/shard_map/all_to_all | solution.py:173
Sparse Core Ops, SparseCore 0:
  21.6 151.3 all-gather.1
  267.4 87.0 reduce-scatter.1
